TPU v7x, 32 devices: a whole 2x2x4 slice. The times are simulated.
32 devices in a mesh: groups: 2 (over x), out: 16 (over z, y, core).
Axes of the slice: x: 2, y: 2, z: 4, core: 2. Of those that a mesh axis runs over, the one named last changes fastest.
Arguments:
- tokens: bfloat16 [256, 8192], P('groups', 'out'), parts along dimension 0, may hold values from -60 to 60, as said below
- grad_hidden: bfloat16 [256, 16384], P('groups', 'out'), parts along dimension 0, may hold values from -6 to 6
- w_gate: bfloat16 [8192, 16384], P(None, 'out'), may hold values from -0.0625 to 0.0625
- w_up: bfloat16 [8192, 16384], P(None, 'out'), may hold values from -0.0625 to 0.0625
- a_factors: bfloat16 [8192, 128], replicated, may hold values from -0.0625 to 0.0625
- b_factors: bfloat16 [2, 64, 16384], P(None, None, 'out'), may hold values from -0.75 to 0.75
- magnitudes: float32 [2, 16384], P(None, 'out'), may hold values from 1 to 2
Outputs:
- hidden: bfloat16 [256, 16384], P('groups', 'out'), parts along dimension 0
- grad_tokens: bfloat16 [256, 8192], P('groups', 'out'), parts along dimension 0
- step_a: float32 [16384, 128], P(('groups', 'out')), parts along dimension 0
- step_b: float32 [4, 64, 16384], P('groups', None, 'out'), parts along dimension 0
- step_m: float32 [4, 16384], P('groups', 'out'), parts along dimension 0
There are 2 independent parts, one for each index of `groups`. A program takes and returns all parts, laid end to end along the dimension named above; an argument that names none is the same for every part. Nothing has to cross between parts.
Inputs may be any that keep to these rules, and one draw needn't show every extreme that they name: `tokens`: activations with feature scales that differ between features.
All inputs are finite; a program needn't handle non-finite values.
Results may differ from a plain program's by a relative error of at most 0.0073.
Values may be sent and summed in bfloat16 or wider, within the bound.
A program may use at most 128 MiB of HBM per device.

v0:
```python
import jax
import jax.numpy as jnp
from jax import lax
from jax.sharding import PartitionSpec as P

D = 8192
FW = 16384
R = 64


def inner_product(left_side, right_side, precision=None):
    return lax.dot_general(
        left_side,
        right_side,
        (((0,), (0,)), ((), ())),
        precision=precision,
        preferred_element_type=jnp.float32,
    )


def outer_contract(left_side, right_side, precision=None):
    return lax.dot_general(
        left_side,
        right_side,
        (((1,), (1,)), ((), ())),
        precision=precision,
        preferred_element_type=jnp.float32,
    )


def split_parts(values):
    upper = values.astype(jnp.bfloat16)
    lower = (values - upper.astype(jnp.float32)).astype(jnp.bfloat16)
    return (upper, lower)


def per_device(tokens, grad_hidden, w_gate, w_up, a_factors, b_factors, magnitudes):
    weights = (w_gate, w_up)
    rank = a_factors.shape[1] // 2
    count_tokens = tokens.shape[0]
    norms = []
    scales = []
    for which in range(2):
        weight = weights[which]
        left = a_factors[:, which * rank : (which + 1) * rank]
        right = b_factors[which]
        merged = weight.astype(jnp.float32) + jnp.dot(
            left, right, preferred_element_type=jnp.float32
        )
        squares = jnp.sum(merged * merged, axis=0)
        norm_col = jnp.sqrt(squares + 1e-06)
        norms.append(norm_col)
        scales.append(magnitudes[which] / norm_col)
    whole = lax.all_gather(tokens, "out", axis=1, tiled=True)
    base_gate = jnp.dot(whole, w_gate, preferred_element_type=jnp.float32)
    base_up = jnp.dot(whole, w_up, preferred_element_type=jnp.float32)
    low_wide = jnp.dot(whole, a_factors, preferred_element_type=jnp.float32)
    low = low_wide.astype(jnp.bfloat16)
    bases = []
    pres = []
    for which, raw in enumerate((base_gate, base_up)):
        base = raw + jnp.dot(
            low[:, which * rank : (which + 1) * rank],
            b_factors[which],
            preferred_element_type=jnp.float32,
        )
        bases.append(base)
        pres.append(base * scales[which][None, :])
    sigma = jax.nn.sigmoid(pres[0])
    hidden = (pres[0] * sigma * pres[1]).astype(jnp.bfloat16)
    cotangent = grad_hidden.astype(jnp.float32)
    dpres = (
        cotangent * pres[1] * sigma * (1.0 + pres[0] * (1.0 - sigma)),
        cotangent * pres[0] * sigma,
    )
    partial_sum = jnp.zeros((count_tokens, w_gate.shape[0]), jnp.float32)
    z_blocks = []
    grad_bs = []
    grad_ms = []
    for which in range(2):
        dscaled = (dpres[which] * scales[which][None, :]).astype(jnp.bfloat16)
        grad_ms.append(jnp.sum(dpres[which] * bases[which], axis=0) / norms[which])
        grad_bs.append(inner_product(low[:, which * rank : (which + 1) * rank], dscaled))
        z_blocks.append(outer_contract(dscaled, b_factors[which]))
        partial_sum = partial_sum + outer_contract(dscaled, weights[which])
    z_local = jnp.concatenate(z_blocks, axis=1)
    z_upper, z_lower = split_parts(z_local)
    partial_sum = (
        partial_sum + outer_contract(z_upper, a_factors) + outer_contract(z_lower, a_factors)
    )
    a_terms = inner_product(whole, z_upper) + inner_product(whole, z_lower)
    grad_a = lax.psum_scatter(a_terms, "out", scatter_dimension=0, tiled=True)
    summed_inputs = lax.psum_scatter(partial_sum, "out", scatter_dimension=1, tiled=True)
    grad_tokens = summed_inputs.astype(jnp.bfloat16)
    grad_b = jnp.stack(grad_bs)
    grad_m = jnp.stack(grad_ms)
    local_energy = jnp.sum(grad_a * grad_a) + jnp.sum(grad_b * grad_b) + jnp.sum(grad_m * grad_m)
    energy = lax.psum(local_energy, "out")
    count_all = 2 * D * R + 2 * R * FW + 2 * FW
    rms_value = jnp.sqrt(energy / count_all + 1e-06)
    return (hidden, grad_tokens, grad_a / rms_value, grad_b / rms_value, grad_m / rms_value)


def solution(mesh):
    in_specs = (
        P("groups", "out"),
        P("groups", "out"),
        P(None, "out"),
        P(None, "out"),
        P(),
        P(None, None, "out"),
        P(None, "out"),
    )
    out_specs = (
        P("groups", "out"),
        P("groups", "out"),
        P(("groups", "out"), None),
        P("groups", None, "out"),
        P("groups", "out"),
    )
    return jax.shard_map(
        per_device, mesh=mesh, in_specs=in_specs, out_specs=out_specs, check_vma=False
    )
```

profile of v0, /device:TPU:0, one launch (start us, length us, event | category | flops | bytes accessed | tf_op | source)
XLA Modules:
  0.0 230.4 jit_solution(6841040627441248489)
XLA Ops:
  7.2 0.7 all-gather.2.cloned.1.call-update
  8.0 8.9 %multiply_reduce_fusion.1 = f32[1024]{0:T(1024)S(1)} fusion(bf16[8192,1024]{1,0:T(8,128)(2,1)} %param.9, bf16[8192,128]{1,0:T(8,128)(2,1)} %param.11, bf16[2,64,1024]{2,1,0:T(8,128)(2,1)} %param.12), kind=kOutput, calls=%fused_computation.1 | convolution fusion | flops 1107295232 | bytes 19009536 | tf_op jit(solution)/shard_map/dot_general | solution.py:47
  16.9 2.9 %copy-done = bf16[8192,1024]{1,0:T(8,128)(2,1)S(1)} copy-done((bf16[8192,1024]{1,0:T(8,128)(2,1)S(1)}, bf16[8192,1024]{1,0:T(8,128)(2,1)}, u32[]{:S(2)}) %copy-start) | copy-done | bytes 16777240
  19.8 5.5 %multiply_reduce_fusion = f32[1024]{0:T(1024)S(1)} fusion(bf16[8192,1024]{1,0:T(8,128)(2,1)S(1)} %copy-done, bf16[8192,128]{1,0:T(8,128)(2,1)S(1)} %copy-done.2, bf16[2,64,1024]{2,1,0:T(8,128)(2,1)S(1)} %copy-done.3), kind=kOutput, calls=%fused_computation | convolution fusion | flops 1107295232 | bytes 19009536 | tf_op jit(solution)/shard_map/dot_general | solution.py:47
  25.4 28.7 %all-gather.2.cloned.1.call-done = bf16[128,8192]{1,0:T(8,128)(2,1)} async-done(((bf16[128,512]{1,0:T(8,128)(2,1)}), bf16[128,8192]{1,0:T(8,128)(2,1)}) %all-gather.2.cloned.1.call-update) | async-done | bytes 2097168 | tf_op jit(solution)/shard_map/all_gather | solution.py:54
  54.1 2.7 %convolution_convert_fusion = bf16[128,128]{0,1:T(8,128)(2,1)S(1)} fusion(bf16[128,8192]{1,0:T(8,128)(2,1)} %all-gather.2.cloned.1.call-done, bf16[8192,128]{1,0:T(8,128)(2,1)S(1)} %copy-done.2), kind=kOutput, calls=%fused_computation.13 | convolution fusion | flops 268451840 | bytes 4227072 | tf_op jit(solution)/shard_map/dot_general | solution.py:57
  56.8 8.9 %fusion.32 = f32[128,1024]{1,0:T(8,128)S(1)} fusion(bf16[128,8192]{1,0:T(8,128)(2,1)} %all-gather.2.cloned.1.call-done, bf16[8192,1024]{1,0:T(8,128)(2,1)} %param.10), kind=kOutput, calls=%fused_computation.62 | convolution fusion | flops 2147483648 | bytes 19398656 | tf_op jit(solution)/shard_map/dot_general | solution.py:56
  65.7 0.2 convolution_add_fusion.4
  66.0 0.8 slice-done.3
  66.8 0.6 copy-done.1
  67.4 2.4 %fusion.31 = f32[128,1024]{1,0:T(8,128)S(1)} fusion(bf16[128,8192]{1,0:T(8,128)(2,1)S(1)} %copy-done.1, bf16[8192,1024]{1,0:T(8,128)(2,1)S(1)} %bitcast.47), kind=kOutput, calls=%fused_computation.61 | convolution fusion | flops 2147483648 | bytes 19398656 | tf_op jit(solution)/shard_map/dot_general | solution.py:55
  69.9 1.3 multiply_reduce_fusion.3
  71.2 0.2 fusion.11
  71.4 0.2 fusion.7
  71.6 0.7 fusion.26
  72.3 2.6 %fusion = f32[8192,128]{0,1:T(8,128)} fusion(f32[128,8192]{1,0:T(8,128)S(1)} %fusion.26, bf16[128,8192]{1,0:T(8,128)(2,1)S(1)} %copy-done.1, f32[128,64]{0,1:T(8,128)S(1)} %fusion.7, f32[128,64]{0,1:T(8,128)S(1)} %fusion.11), kind=kOutput, calls=%fused_computation.3 | convolution fusion | flops 269565952 | bytes 10551296 | tf_op jit(solution)/shard_map/dot_general | solution.py:12
  75.0 0.3 reduce-scatter.3.cloned.1.call-start
  75.3 13.5 %fusion.33 = f32[128,8192]{1,0:T(8,128)} fusion(bf16[128,1024]{1,0:T(8,128)(2,1)S(1)} %get-tuple-element.12, bf16[8192,1024]{1,0:T(8,128)(2,1)} %param.9), kind=kOutput, calls=%fused_computation.63 | convolution fusion | flops 2147483648 | bytes 21233664 | tf_op jit(solution)/shard_map/dot_general | solution.py:22
  88.8 15.3 %convolution_add_fusion.3 = f32[128,8192]{1,0:T(8,128)} fusion(f32[128,8192]{1,0:T(8,128)} %fusion.33, bf16[128,1024]{1,0:T(8,128)(2,1)S(1)} %get-tuple-element.14, bf16[8192,1024]{1,0:T(8,128)(2,1)} %param.10), kind=kOutput, calls=%fused_computation.6 | convolution fusion | flops 2148532224 | bytes 25427968 | tf_op jit(solution)/shard_map/dot_general | solution.py:22
  104.1 3.0 %convolution_add_fusion.2 = f32[128,8192]{1,0:T(8,128)S(1)} fusion(f32[128,8192]{1,0:T(8,128)} %convolution_add_fusion.3, bf16[8192,128]{1,0:T(8,128)(2,1)S(1)} %copy-done.2, f32[128,64]{0,1:T(8,128)S(1)} %fusion.7, f32[128,64]{0,1:T(8,128)S(1)} %fusion.11), kind=kOutput, calls=%fused_computation.5 | convolution fusion | flops 269549568 | bytes 10551296 | tf_op jit(solution)/shard_map/dot_general | solution.py:22
  107.1 2.8 %convolution_add_fusion.1 = f32[128,8192]{1,0:T(8,128)} fusion(f32[128,8192]{1,0:T(8,128)S(1)} %convolution_add_fusion.2, bf16[8192,128]{1,0:T(8,128)(2,1)S(1)} %copy-done.2, f32[128,64]{0,1:T(8,128)S(1)} %fusion.7, f32[128,64]{0,1:T(8,128)S(1)} %fusion.11), kind=kOutput, calls=%fused_computation.4 | convolution fusion | flops 269565952 | bytes 10551296 | tf_op jit(solution)/shard_map/dot_general | solution.py:22
  109.9 0.6 multiply_reduce_fusion.6
  110.9 0.7 multiply_reduce_fusion.4
  111.6 34.9 %reduce-scatter.5.cloned.1.call-done = f32[512,128]{0,1:T(8,128)} async-done(((f32[8192,128]{0,1:T(8,128)}), f32[512,128]{0,1:T(8,128)}) %reduce-scatter.5.cloned.1.call-update) | async-done | bytes 262160 | tf_op jit(solution)/shard_map/reduce_scatter | solution.py:92
  146.5 1.6 multiply_reduce_fusion.5
  150.1 30.5 %psum.7 = f32[]{:T(128)} all-reduce(f32[]{:T(128)S(6)} %add.92), channel_id=1, replica_groups=mesh['groups'=2,'out'=16] {'out'}, use_global_device_ids=true, to_apply=%region_9.0 | all-reduce | flops 1 | bytes 8 | tf_op jit(solution)/shard_map/psum | solution.py:98
  181.3 1.0 broadcast_divide_fusion
  182.3 0.8 copy.12
  183.1 0.6 broadcast_divide_fusion.1
  183.8 0.9 fusion.6
  184.6 37.7 %reduce-scatter.3.cloned.1.call-done = f32[128,512]{1,0:T(8,128)} async-done(((f32[128,8192]{1,0:T(8,128)}), f32[128,512]{1,0:T(8,128)}) %reduce-scatter.3.cloned.1.call-update) | async-done | bytes 262160 | tf_op jit(solution)/shard_map/reduce_scatter | solution.py:93
  222.3 1.6 convert_element_type.43
  (29 shorter events, 0.5 us)
Async XLA Ops:
  7.2 46.9 %all-gather.2.cloned.1.call-start = ((), (), s32[]{:S(2)}) async-start(), calls=%async_computation.2 | async-start | bytes 2228224 | tf_op jit(solution)/shard_map/all_gather | solution.py:54
  7.9 9.0 %copy-start.2 = (bf16[8192,128]{1,0:T(8,128)(2,1)S(1)}, bf16[8192,128]{1,0:T(8,128)(2,1)}, u32[]{:S(2)}) copy-start(bf16[8192,128]{1,0:T(8,128)(2,1)} %param.11) | copy-start | bytes 6291460
  7.9 9.0 %copy-start.3 = (bf16[2,64,1024]{2,1,0:T(8,128)(2,1)S(1)}, bf16[2,64,1024]{2,1,0:T(8,128)(2,1)}, u32[]{:S(2)}) copy-start(bf16[2,64,1024]{2,1,0:T(8,128)(2,1)} %param.12) | copy-start | bytes 786436
  7.9 138.6 %reduce-scatter.5.cloned.1.call-start = ((), (), s32[]{:S(2)}) async-start(), calls=%async_computation.4 | async-start | bytes 4456448 | tf_op jit(solution)/shard_map/reduce_scatter | solution.py:92
  8.0 11.9 %copy-start = (bf16[8192,1024]{1,0:T(8,128)(2,1)S(1)}, bf16[8192,1024]{1,0:T(8,128)(2,1)}, u32[]{:S(2)}) copy-start(bf16[8192,1024]{1,0:T(8,128)(2,1)} %param.10) | copy-start | bytes 50331652
  19.8 5.6 %copy-start.4 = (f32[2,1024]{1,0:T(2,128)S(1)}, f32[2,1024]{1,0:T(2,128)}, u32[]{:S(2)}) copy-start(f32[2,1024]{1,0:T(2,128)} %param.13) | copy-start | bytes 24580
  54.1 11.9 %slice-start = ((s8[16777216]{0:T(1024)(128)(4,1)}), s8[4194304]{0:T(1024)(128)(4,1)S(1)}, s32[]{:S(2)}) async-start(s8[16777216]{0:T(1024)(128)(4,1)} %bitcast.46), calls=%async_computation.5 | async-start | bytes 8388608
  56.8 9.2 %slice-start.1 = ((s8[16777216]{0:T(1024)(128)(4,1)}), s8[4194304]{0:T(1024)(128)(4,1)S(1)}, s32[]{:S(2)}) async-start(s8[16777216]{0:T(1024)(128)(4,1)} %bitcast.46), calls=%async_computation.6 | async-start | bytes 8388608
  56.8 9.2 %slice-start.2 = ((s8[16777216]{0:T(1024)(128)(4,1)}), s8[4194304]{0:T(1024)(128)(4,1)S(1)}, s32[]{:S(2)}) async-start(s8[16777216]{0:T(1024)(128)(4,1)} %bitcast.46), calls=%async_computation.7 | async-start | bytes 8388608
  56.8 10.0 %slice-start.3 = ((s8[16777216]{0:T(1024)(128)(4,1)}), s8[4194304]{0:T(1024)(128)(4,1)S(1)}, s32[]{:S(2)}) async-start(s8[16777216]{0:T(1024)(128)(4,1)} %bitcast.46), calls=%async_computation.8 | async-start | bytes 8388608
  56.8 10.6 %copy-start.1 = (bf16[128,8192]{1,0:T(8,128)(2,1)S(1)}, bf16[128,8192]{1,0:T(8,128)(2,1)}, u32[]{:S(2)}) copy-start(bf16[128,8192]{1,0:T(8,128)(2,1)} %all-gather.2.cloned.1.call-done) | copy-start | bytes 6291460
  67.4 2.5 %copy-start.5 = (bf16[128,1024]{1,0:T(8,128)(2,1)S(1)}, bf16[128,1024]{1,0:T(8,128)(2,1)}, u32[]{:S(2)}) copy-start(bf16[128,1024]{1,0:T(8,128)(2,1)} %param.8) | copy-start | bytes 786436
  75.0 147.3 %reduce-scatter.3.cloned.1.call-start = ((), (), s32[]{:S(2)}) async-start(), calls=%async_computation.3 | async-start | bytes 4456448 | tf_op jit(solution)/shard_map/reduce_scatter | solution.py:93
Sparse Core Ops, SparseCore 0:
  10.2 43.8 all-gather.1
  75.1 71.3 reduce-scatter.4
  150.9 71.3 reduce-scatter.2
where the time goes:
time: 231 us; the launch traced here: 230 us
  waiting for transfers between devices  102 us (44%)
  matrix products  68.7 us (30%)
  blocking collectives  30.5 us (13%)
  between operations  16.6 us (7%)
  other arithmetic  7.07 us (3%)
  local copies, waits for them, and re-layouts  5.15 us (2%)
    reduce_scatter x1, waiting for transfers between devices, per_device(): lax.psum_scatter(partial_sum, 'out', scatter_dimension=1, tiled=True)  37.7 us
    dot_general x6, matrix products, outer_contract(): lax.dot_general(left_side, right_side, (((1,), (1,)), ((), ())), precisio...  35 us
    reduce_scatter x1, waiting for transfers between devices, per_device(): grad_a = lax.psum_scatter(a_terms, 'out', scatter_dimension=0, tiled=True)  34.9 us
    psum x1, blocking collectives, per_device(): energy = lax.psum(local_energy, 'out')  30.5 us
    all_gather x1, waiting for transfers between devices, per_device(): whole = lax.all_gather(tokens, 'out', axis=1, tiled=True)  28.7 us
    dot_general x2, matrix products, per_device(): jnp.dot(left, right, preferred_element_type=jnp.float32)  14.5 us
    dot_general x1, matrix products, per_device(): base_up = jnp.dot(whole, w_up, preferred_element_type=jnp.float32)  8.88 us
    unnamed x21, local copies, waits for them, and re-layouts  5.15 us
  transfers between devices with their start and end apart: 3, of which 3 were waited for; matrix products, arithmetic and copies ran while one was open for 24% of the time, Pallas kernels for 0%

commit v1 on v0

--- a/solution.py
+++ b/solution.py
@@ -6,6 +6,22 @@
 D = 8192
 FW = 16384
 R = 64
+
+
+def ring_gather(x, axis, dim):
+    ways, here, step = (lax.axis_size(axis), lax.axis_index(axis), x.shape[dim])
+    lengths = [n * ways if d == dim else n for d, n in enumerate(x.shape)]
+    full = lax.dynamic_update_slice_in_dim(jnp.zeros(lengths, x.dtype), x, here * step, axis=dim)
+    going_up = going_down = x
+    for far in range(1, ways // 2 + 1):
+        going_up = lax.ppermute(going_up, axis, [(d, (d + 1) % ways) for d in range(ways)])
+        full = lax.dynamic_update_slice_in_dim(full, going_up, (here - far) % ways * step, axis=dim)
+        if 2 * far < ways:
+            going_down = lax.ppermute(going_down, axis, [(d, (d - 1) % ways) for d in range(ways)])
+            full = lax.dynamic_update_slice_in_dim(
+                full, going_down, (here + far) % ways * step, axis=dim
+            )
+    return full
 
 
 def inner_product(left_side, right_side, precision=None):
@@ -51,7 +67,7 @@
         norm_col = jnp.sqrt(squares + 1e-06)
         norms.append(norm_col)
         scales.append(magnitudes[which] / norm_col)
-    whole = lax.all_gather(tokens, "out", axis=1, tiled=True)
+    whole = ring_gather(tokens, "out", 1)
     base_gate = jnp.dot(whole, w_gate, preferred_element_type=jnp.float32)
     base_up = jnp.dot(whole, w_up, preferred_element_type=jnp.float32)
     low_wide = jnp.dot(whole, a_factors, preferred_element_type=jnp.float32)

time: 231 us -> 253 us (1.095)
  starting transfers between devices: 0.34 us -> 32.7 us
  waiting for transfers between devices: 102 us -> 95.7 us
  local copies, waits for them, and re-layouts: 5.15 us -> 1.84 us
    ppermute x0 -> x15, starting transfers between devices: none -> 32.4 us  [the longest x7 31.8 us: ring_gather(): lax.ppermute(going_down, axis, [(d, (d - 1) % ways) for d in range(ways)])]
    all_gather x1 -> x0, waiting for transfers between devices: 28.7 us -> none  [per_device(): whole = lax.all_gather(tokens, 'out', axis=1, tiled=True)]
    ppermute x0 -> x15, waiting for transfers between devices: none -> 23 us  [the longest x8 23 us: ring_gather(): lax.ppermute(going_up, axis, [(d, (d + 1) % ways) for d in range(ways)])]
    unnamed x21 -> x20, local copies, waits for them, and re-layouts: 5.15 us -> 1.42 us
  transfers between devices with their start and end apart: 3 -> 17, of which waited for: 3 -> 9; matrix products, arithmetic and copies ran while one was open for 24% -> 22% of each run, Pallas kernels for 0% -> 0%
where the time goes in v1:
time: 253 us; the launch traced here: 252 us
  waiting for transfers between devices  95.7 us (38%)
  matrix products  66.5 us (26%)
  starting transfers between devices  32.7 us (13%)
  blocking collectives  30.6 us (12%)
  between operations  17.4 us (7%)
  other arithmetic  7.77 us (3%)
    reduce_scatter x1, waiting for transfers between devices, per_device(): lax.psum_scatter(partial_sum, 'out', scatter_dimension=1, tiled=True)  38 us
    dot_general x6, matrix products, outer_contract(): lax.dot_general(left_side, right_side, (((1,), (1,)), ((), ())), precisio...  35 us
    reduce_scatter x1, waiting for transfers between devices, per_device(): grad_a = lax.psum_scatter(a_terms, 'out', scatter_dimension=0, tiled=True)  34.7 us
    ppermute x7, starting transfers between devices, ring_gather(): lax.ppermute(going_down, axis, [(d, (d - 1) % ways) for d in range(ways)])  31.8 us
    psum x1, blocking collectives, per_device(): energy = lax.psum(local_energy, 'out')  30.6 us
    ppermute x8, waiting for transfers between devices, ring_gather(): lax.ppermute(going_up, axis, [(d, (d + 1) % ways) for d in range(ways)])  23 us
    dot_general x2, matrix products, per_device(): jnp.dot(left, right, preferred_element_type=jnp.float32)  14.1 us
    dot_general x1, matrix products, per_device(): base_up = jnp.dot(whole, w_up, preferred_element_type=jnp.float32)  8.43 us
  transfers between devices with their start and end apart: 17, of which 9 were waited for; matrix products, arithmetic and copies ran while one was open for 22% of the time, Pallas kernels for 0%

profile of v1, /device:TPU:0, one launch (start us, length us, event | category | flops | bytes accessed | tf_op | source)
XLA Modules:
  0.0 252.4 jit_solution(1906558172333029101)
XLA Ops:
  7.7 5.1 %collective-permute-start.1 = (bf16[128,512]{1,0:T(8,128)(2,1)}, bf16[128,512]{1,0:T(8,128)(2,1)S(1)}, u32[]{:S(2)}, u32[]{:S(2)}) collective-permute-start(bf16[128,512]{1,0:T(8,128)(2,1)} %param.7), channel_id=1, source_target_pairs={{0,15},{1,0},{2,1},{3,2},{4,3},{5,4},{6,5},{7,6},{8,7},{9,8},{10,9... | collective-permute-start | bytes 393224 | tf_op jit(solution)/shard_map/ppermute | solution.py:20
  12.8 8.8 %multiply_reduce_fusion.1 = f32[1024]{0:T(1024)S(1)} fusion(bf16[8192,1024]{1,0:T(8,128)(2,1)} %param.9, bf16[8192,128]{1,0:T(8,128)(2,1)} %param.11, bf16[2,64,1024]{2,1,0:T(8,128)(2,1)} %param.12), kind=kOutput, calls=%fused_computation.1 | convolution fusion | flops 1107295232 | bytes 19009536 | tf_op jit(solution)/shard_map/dot_general | solution.py:63
  21.7 5.3 %multiply_reduce_fusion = f32[1024]{0:T(1024)S(1)} fusion(bf16[8192,1024]{1,0:T(8,128)(2,1)S(1)} %copy-done, bf16[8192,128]{1,0:T(8,128)(2,1)S(1)} %copy-done.1, bf16[2,64,1024]{2,1,0:T(8,128)(2,1)S(1)} %copy-done.2), kind=kOutput, calls=%fused_computation | convolution fusion | flops 1107295232 | bytes 19009536 | tf_op jit(solution)/shard_map/dot_general | solution.py:63
  28.0 4.4 %collective-permute-start.3 = (bf16[128,512]{1,0:T(8,128)(2,1)S(1)}, bf16[128,512]{1,0:T(8,128)(2,1)S(1)}, u32[]{:S(2)}, u32[]{:S(2)}) collective-permute-start(bf16[128,512]{1,0:T(8,128)(2,1)S(1)} %collective-permute-done.1), channel_id=1, source_target_pairs={{0,15},{1,0},{2,1},{3,2},{4,3},{5,4},{6,5},{7,6},{8,7},{9,8},{10,9... | collective-permute-start | bytes 393224 | tf_op jit(solution)/shard_map/ppermute | solution.py:20
  32.5 2.6 %collective-permute-done.2 = bf16[128,512]{1,0:T(8,128)(2,1)S(1)} collective-permute-done((bf16[128,512]{1,0:T(8,128)(2,1)S(1)}, bf16[128,512]{1,0:T(8,128)(2,1)S(1)}, u32[]{:S(2)}, u32[]{:S(2)}) %collective-permute-start.2) | collective-permute-done | bytes 131104 | tf_op jit(solution)/shard_map/ppermute | solution.py:17
  35.1 4.5 %collective-permute-start.5 = (bf16[128,512]{1,0:T(8,128)(2,1)S(1)}, bf16[128,512]{1,0:T(8,128)(2,1)S(1)}, u32[]{:S(2)}, u32[]{:S(2)}) collective-permute-start(bf16[128,512]{1,0:T(8,128)(2,1)S(1)} %collective-permute-done.3), channel_id=1, source_target_pairs={{0,15},{1,0},{2,1},{3,2},{4,3},{5,4},{6,5},{7,6},{8,7},{9,8},{10,9... | collective-permute-start | bytes 393224 | tf_op jit(solution)/shard_map/ppermute | solution.py:20
  39.7 2.6 %collective-permute-done.4 = bf16[128,512]{1,0:T(8,128)(2,1)S(1)} collective-permute-done((bf16[128,512]{1,0:T(8,128)(2,1)S(1)}, bf16[128,512]{1,0:T(8,128)(2,1)S(1)}, u32[]{:S(2)}, u32[]{:S(2)}) %collective-permute-start.4) | collective-permute-done | bytes 131104 | tf_op jit(solution)/shard_map/ppermute | solution.py:17
  42.3 4.4 %collective-permute-start.7 = (bf16[128,512]{1,0:T(8,128)(2,1)S(1)}, bf16[128,512]{1,0:T(8,128)(2,1)S(1)}, u32[]{:S(2)}, u32[]{:S(2)}) collective-permute-start(bf16[128,512]{1,0:T(8,128)(2,1)S(1)} %collective-permute-done.5), channel_id=1, source_target_pairs={{0,15},{1,0},{2,1},{3,2},{4,3},{5,4},{6,5},{7,6},{8,7},{9,8},{10,9... | collective-permute-start | bytes 393224 | tf_op jit(solution)/shard_map/ppermute | solution.py:20
  46.8 2.7 %collective-permute-done.6 = bf16[128,512]{1,0:T(8,128)(2,1)S(1)} collective-permute-done((bf16[128,512]{1,0:T(8,128)(2,1)S(1)}, bf16[128,512]{1,0:T(8,128)(2,1)S(1)}, u32[]{:S(2)}, u32[]{:S(2)}) %collective-permute-start.6) | collective-permute-done | bytes 131104 | tf_op jit(solution)/shard_map/ppermute | solution.py:17
  49.5 4.4 %collective-permute-start.9 = (bf16[128,512]{1,0:T(8,128)(2,1)S(1)}, bf16[128,512]{1,0:T(8,128)(2,1)S(1)}, u32[]{:S(2)}, u32[]{:S(2)}) collective-permute-start(bf16[128,512]{1,0:T(8,128)(2,1)S(1)} %collective-permute-done.7), channel_id=1, source_target_pairs={{0,15},{1,0},{2,1},{3,2},{4,3},{5,4},{6,5},{7,6},{8,7},{9,8},{10,9... | collective-permute-start | bytes 393224 | tf_op jit(solution)/shard_map/ppermute | solution.py:20
  54.0 2.7 %collective-permute-done.8 = bf16[128,512]{1,0:T(8,128)(2,1)S(1)} collective-permute-done((bf16[128,512]{1,0:T(8,128)(2,1)S(1)}, bf16[128,512]{1,0:T(8,128)(2,1)S(1)}, u32[]{:S(2)}, u32[]{:S(2)}) %collective-permute-start.8) | collective-permute-done | bytes 131104 | tf_op jit(solution)/shard_map/ppermute | solution.py:17
  56.7 4.4 %collective-permute-start.11 = (bf16[128,512]{1,0:T(8,128)(2,1)S(1)}, bf16[128,512]{1,0:T(8,128)(2,1)S(1)}, u32[]{:S(2)}, u32[]{:S(2)}) collective-permute-start(bf16[128,512]{1,0:T(8,128)(2,1)S(1)} %collective-permute-done.9), channel_id=1, source_target_pairs={{0,15},{1,0},{2,1},{3,2},{4,3},{5,4},{6,5},{7,6},{8,7},{9,8},{10,9... | collective-permute-start | bytes 393224 | tf_op jit(solution)/shard_map/ppermute | solution.py:20
  61.2 2.7 %collective-permute-done.10 = bf16[128,512]{1,0:T(8,128)(2,1)S(1)} collective-permute-done((bf16[128,512]{1,0:T(8,128)(2,1)S(1)}, bf16[128,512]{1,0:T(8,128)(2,1)S(1)}, u32[]{:S(2)}, u32[]{:S(2)}) %collective-permute-start.10) | collective-permute-done | bytes 131104 | tf_op jit(solution)/shard_map/ppermute | solution.py:17
  63.9 4.4 %collective-permute-start.13 = (bf16[128,512]{1,0:T(8,128)(2,1)S(1)}, bf16[128,512]{1,0:T(8,128)(2,1)S(1)}, u32[]{:S(2)}, u32[]{:S(2)}) collective-permute-start(bf16[128,512]{1,0:T(8,128)(2,1)S(1)} %collective-permute-done.11), channel_id=1, source_target_pairs={{0,15},{1,0},{2,1},{3,2},{4,3},{5,4},{6,5},{7,6},{8,7},{9,8},{10,9... | collective-permute-start | bytes 393224 | tf_op jit(solution)/shard_map/ppermute | solution.py:20
  68.4 2.6 %collective-permute-done.12 = bf16[128,512]{1,0:T(8,128)(2,1)S(1)} collective-permute-done((bf16[128,512]{1,0:T(8,128)(2,1)S(1)}, bf16[128,512]{1,0:T(8,128)(2,1)S(1)}, u32[]{:S(2)}, u32[]{:S(2)}) %collective-permute-start.12) | collective-permute-done | bytes 131104 | tf_op jit(solution)/shard_map/ppermute | solution.py:17
  71.0 7.0 %collective-permute-done.14 = bf16[128,512]{1,0:T(8,128)(2,1)S(1)} collective-permute-done((bf16[128,512]{1,0:T(8,128)(2,1)S(1)}, bf16[128,512]{1,0:T(8,128)(2,1)S(1)}, u32[]{:S(2)}, u32[]{:S(2)}) %collective-permute-start.14) | collective-permute-done | bytes 131104 | tf_op jit(solution)/shard_map/ppermute | solution.py:17
  78.1 1.0 convolution_convert_fusion
  79.6 8.4 %convolution_add_fusion.4 = f32[128,1024]{1,0:T(8,128)S(1)} fusion(f32[128,1024]{1,0:T(8,128)S(1)} %fusion.9, bf16[128,8192]{1,0:T(8,128)(2,1)S(1)} %constant_dynamic-update-slice_fusion, bf16[8192,1024]{1,0:T(8,128)(2,1)} %param.10), kind=kOutput, calls=%fused_computation.8 | convolution fusion | flops 2147614720 | bytes 19922944 | tf_op jit(solution)/shard_map/dot_general | solution.py:72
  88.1 1.0 slice-done.3
  89.1 3.6 %multiply_reduce_fusion.3 = (f32[1024]{0:T(1024)S(1)}, f32[1024]{0:T(1024)S(1)}, bf16[128,1024]{1,0:T(8,128)(2,1)S(1)}, bf16[128,1024]{1,0:T(8,128)(2,1)}, bf16[128,1024]{1,0:T(8,128)(2,1)S(1)}) fusion(f32[1024]{0:T(1024)S(1)} %bitcast.50, f32[128,1024]{1,0:T(8,128)S(1)} %convolution_add_fusion.4, f32[1024]{0:T(1024)S(1)} %bitcast.51, ...), kind=kOutput, calls=%fused_computation.20 | convolution fusion | flops 2150889472 | bytes 20987904 | tf_op jit(solution)/shard_map/dot_general | solution.py:71
  93.9 2.8 %convolution_add_fusion = f32[8192,128]{1,0:T(8,128)} fusion(f32[8192,128]{1,0:T(8,128)S(1)} %fusion.31, bf16[128,8192]{1,0:T(8,128)(2,1)S(1)} %constant_dynamic-update-slice_fusion, f32[128,64]{0,1:T(8,128)S(1)} %fusion.6, f32[128,64]{0,1:T(8,128)S(1)} %fusion.11), kind=kOutput, calls=%fused_computation.2 | convolution fusion | flops 269549568 | bytes 10551296 | tf_op jit(solution)/shard_map/dot_general | solution.py:28
  97.0 13.6 %fusion.32 = f32[128,8192]{1,0:T(8,128)} fusion(bf16[128,1024]{1,0:T(8,128)(2,1)S(1)} %get-tuple-element.7, bf16[8192,1024]{1,0:T(8,128)(2,1)} %param.9), kind=kOutput, calls=%fused_computation.78 | convolution fusion | flops 2147483648 | bytes 21233664 | tf_op jit(solution)/shard_map/dot_general | solution.py:38
  110.6 15.2 %convolution_add_fusion.3 = f32[128,8192]{1,0:T(8,128)} fusion(f32[128,8192]{1,0:T(8,128)} %fusion.32, bf16[128,1024]{1,0:T(8,128)(2,1)S(1)} %get-tuple-element.9, bf16[8192,1024]{1,0:T(8,128)(2,1)} %param.10), kind=kOutput, calls=%fused_computation.5 | convolution fusion | flops 2148532224 | bytes 25427968 | tf_op jit(solution)/shard_map/dot_general | solution.py:38
  125.8 2.9 %convolution_add_fusion.2 = f32[128,8192]{1,0:T(8,128)S(1)} fusion(f32[128,8192]{1,0:T(8,128)} %convolution_add_fusion.3, bf16[8192,128]{1,0:T(8,128)(2,1)S(1)} %copy-done.1, f32[128,64]{0,1:T(8,128)S(1)} %fusion.6, f32[128,64]{0,1:T(8,128)S(1)} %fusion.11), kind=kOutput, calls=%fused_computation.4 | convolution fusion | flops 269549568 | bytes 10551296 | tf_op jit(solution)/shard_map/dot_general | solution.py:38
  128.7 2.8 %convolution_add_fusion.1 = f32[128,8192]{1,0:T(8,128)} fusion(f32[128,8192]{1,0:T(8,128)S(1)} %convolution_add_fusion.2, bf16[8192,128]{1,0:T(8,128)(2,1)S(1)} %copy-done.1, f32[128,64]{0,1:T(8,128)S(1)} %fusion.6, f32[128,64]{0,1:T(8,128)S(1)} %fusion.11), kind=kOutput, calls=%fused_computation.3 | convolution fusion | flops 269565952 | bytes 10551296 | tf_op jit(solution)/shard_map/dot_general | solution.py:38
  133.3 34.7 %reduce-scatter.5.cloned.1.call-done = f32[512,128]{1,0:T(8,128)} async-done(((f32[8192,128]{1,0:T(8,128)}), f32[512,128]{1,0:T(8,128)}) %reduce-scatter.5.cloned.1.call-update) | async-done | bytes 262160 | tf_op jit(solution)/shard_map/reduce_scatter | solution.py:108
  168.0 1.6 multiply_reduce_fusion.5
  171.5 30.6 %psum.7 = f32[]{:T(128)} all-reduce(f32[]{:T(128)S(6)} %add.249), channel_id=1, replica_groups=mesh['groups'=2,'out'=16] {'out'}, use_global_device_ids=true, to_apply=%region_9.10 | all-reduce | flops 1 | bytes 8 | tf_op jit(solution)/shard_map/psum | solution.py:114
  203.4 0.8 fusion.5
  204.3 1.7 broadcast_divide_fusion
  205.9 38.0 %reduce-scatter.3.cloned.1.call-done = f32[128,512]{1,0:T(8,128)} async-done(((f32[128,8192]{1,0:T(8,128)}), f32[128,512]{1,0:T(8,128)}) %reduce-scatter.3.cloned.1.call-update) | async-done | bytes 262160 | tf_op jit(solution)/shard_map/reduce_scatter | solution.py:109
  244.0 1.6 convert_element_type.43
  (72 shorter events, 5.8 us)
Async XLA Ops:
  7.2 14.4 %copy-start.1 = (bf16[8192,128]{1,0:T(8,128)(2,1)S(1)}, bf16[8192,128]{1,0:T(8,128)(2,1)}, u32[]{:S(2)}) copy-start(bf16[8192,128]{1,0:T(8,128)(2,1)} %param.11) | copy-start | bytes 6291460
  7.2 14.4 %copy-start.2 = (bf16[2,64,1024]{2,1,0:T(8,128)(2,1)S(1)}, bf16[2,64,1024]{2,1,0:T(8,128)(2,1)}, u32[]{:S(2)}) copy-start(bf16[2,64,1024]{2,1,0:T(8,128)(2,1)} %param.12) | copy-start | bytes 786436
  7.2 160.8 %reduce-scatter.5.cloned.1.call-start = ((), (), s32[]{:S(2)}) async-start(), calls=%async_computation.3 | async-start | bytes 4456448 | tf_op jit(solution)/shard_map/reduce_scatter | solution.py:108
  7.2 14.4 %copy-start = (bf16[8192,1024]{1,0:T(8,128)(2,1)S(1)}, bf16[8192,1024]{1,0:T(8,128)(2,1)}, u32[]{:S(2)}) copy-start(bf16[8192,1024]{1,0:T(8,128)(2,1)} %param.10) | copy-start | bytes 50331652
  7.2 20.7 %collective-permute-start = (bf16[128,512]{1,0:T(8,128)(2,1)}, bf16[128,512]{1,0:T(8,128)(2,1)S(1)}, u32[]{:S(2)}, u32[]{:S(2)}) collective-permute-start(bf16[128,512]{1,0:T(8,128)(2,1)} %param.7), channel_id=1, source_target_pairs={{0,1},{1,2},{2,3},{3,4},{4,5},{5,6},{6,7},{7,8},{8,9},{9,10},{10,1... | collective-permute-start | bytes 393224 | tf_op jit(solution)/shard_map/ppermute | solution.py:17
  7.7 20.3 %collective-permute-start.1 = (bf16[128,512]{1,0:T(8,128)(2,1)}, bf16[128,512]{1,0:T(8,128)(2,1)S(1)}, u32[]{:S(2)}, u32[]{:S(2)}) collective-permute-start(bf16[128,512]{1,0:T(8,128)(2,1)} %param.7), channel_id=1, source_target_pairs={{0,15},{1,0},{2,1},{3,2},{4,3},{5,4},{6,5},{7,6},{8,7},{9,8},{10,9... | collective-permute-start | bytes 393224 | tf_op jit(solution)/shard_map/ppermute | solution.py:20
  21.6 5.4 %copy-start.4 = (f32[2,1024]{1,0:T(2,128)S(1)}, f32[2,1024]{1,0:T(2,128)}, u32[]{:S(2)}) copy-start(f32[2,1024]{1,0:T(2,128)} %param.13) | copy-start | bytes 24580
  27.0 0.9 copy-start.3
  27.9 7.1 %collective-permute-start.2 = (bf16[128,512]{1,0:T(8,128)(2,1)S(1)}, bf16[128,512]{1,0:T(8,128)(2,1)S(1)}, u32[]{:S(2)}, u32[]{:S(2)}) collective-permute-start(bf16[128,512]{1,0:T(8,128)(2,1)S(1)} %collective-permute-done), channel_id=1, source_target_pairs={{0,1},{1,2},{2,3},{3,4},{4,5},{5,6},{6,7},{7,8},{8,9},{9,10},{10,1... | collective-permute-start | bytes 393224 | tf_op jit(solution)/shard_map/ppermute | solution.py:17
  28.0 7.1 %collective-permute-start.3 = (bf16[128,512]{1,0:T(8,128)(2,1)S(1)}, bf16[128,512]{1,0:T(8,128)(2,1)S(1)}, u32[]{:S(2)}, u32[]{:S(2)}) collective-permute-start(bf16[128,512]{1,0:T(8,128)(2,1)S(1)} %collective-permute-done.1), channel_id=1, source_target_pairs={{0,15},{1,0},{2,1},{3,2},{4,3},{5,4},{6,5},{7,6},{8,7},{9,8},{10,9... | collective-permute-start | bytes 393224 | tf_op jit(solution)/shard_map/ppermute | solution.py:20
  35.1 7.2 %collective-permute-start.4 = (bf16[128,512]{1,0:T(8,128)(2,1)S(1)}, bf16[128,512]{1,0:T(8,128)(2,1)S(1)}, u32[]{:S(2)}, u32[]{:S(2)}) collective-permute-start(bf16[128,512]{1,0:T(8,128)(2,1)S(1)} %collective-permute-done.2), channel_id=1, source_target_pairs={{0,1},{1,2},{2,3},{3,4},{4,5},{5,6},{6,7},{7,8},{8,9},{9,10},{10,1... | collective-permute-start | bytes 393224 | tf_op jit(solution)/shard_map/ppermute | solution.py:17
  35.1 7.2 %collective-permute-start.5 = (bf16[128,512]{1,0:T(8,128)(2,1)S(1)}, bf16[128,512]{1,0:T(8,128)(2,1)S(1)}, u32[]{:S(2)}, u32[]{:S(2)}) collective-permute-start(bf16[128,512]{1,0:T(8,128)(2,1)S(1)} %collective-permute-done.3), channel_id=1, source_target_pairs={{0,15},{1,0},{2,1},{3,2},{4,3},{5,4},{6,5},{7,6},{8,7},{9,8},{10,9... | collective-permute-start | bytes 393224 | tf_op jit(solution)/shard_map/ppermute | solution.py:20
  42.3 7.2 %collective-permute-start.6 = (bf16[128,512]{1,0:T(8,128)(2,1)S(1)}, bf16[128,512]{1,0:T(8,128)(2,1)S(1)}, u32[]{:S(2)}, u32[]{:S(2)}) collective-permute-start(bf16[128,512]{1,0:T(8,128)(2,1)S(1)} %collective-permute-done.4), channel_id=1, source_target_pairs={{0,1},{1,2},{2,3},{3,4},{4,5},{5,6},{6,7},{7,8},{8,9},{9,10},{10,1... | collective-permute-start | bytes 393224 | tf_op jit(solution)/shard_map/ppermute | solution.py:17
  42.3 7.2 %collective-permute-start.7 = (bf16[128,512]{1,0:T(8,128)(2,1)S(1)}, bf16[128,512]{1,0:T(8,128)(2,1)S(1)}, u32[]{:S(2)}, u32[]{:S(2)}) collective-permute-start(bf16[128,512]{1,0:T(8,128)(2,1)S(1)} %collective-permute-done.5), channel_id=1, source_target_pairs={{0,15},{1,0},{2,1},{3,2},{4,3},{5,4},{6,5},{7,6},{8,7},{9,8},{10,9... | collective-permute-start | bytes 393224 | tf_op jit(solution)/shard_map/ppermute | solution.py:20
  49.5 7.2 %collective-permute-start.8 = (bf16[128,512]{1,0:T(8,128)(2,1)S(1)}, bf16[128,512]{1,0:T(8,128)(2,1)S(1)}, u32[]{:S(2)}, u32[]{:S(2)}) collective-permute-start(bf16[128,512]{1,0:T(8,128)(2,1)S(1)} %collective-permute-done.6), channel_id=1, source_target_pairs={{0,1},{1,2},{2,3},{3,4},{4,5},{5,6},{6,7},{7,8},{8,9},{9,10},{10,1... | collective-permute-start | bytes 393224 | tf_op jit(solution)/shard_map/ppermute | solution.py:17
  49.5 7.2 %collective-permute-start.9 = (bf16[128,512]{1,0:T(8,128)(2,1)S(1)}, bf16[128,512]{1,0:T(8,128)(2,1)S(1)}, u32[]{:S(2)}, u32[]{:S(2)}) collective-permute-start(bf16[128,512]{1,0:T(8,128)(2,1)S(1)} %collective-permute-done.7), channel_id=1, source_target_pairs={{0,15},{1,0},{2,1},{3,2},{4,3},{5,4},{6,5},{7,6},{8,7},{9,8},{10,9... | collective-permute-start | bytes 393224 | tf_op jit(solution)/shard_map/ppermute | solution.py:20
  56.7 7.2 %collective-permute-start.10 = (bf16[128,512]{1,0:T(8,128)(2,1)S(1)}, bf16[128,512]{1,0:T(8,128)(2,1)S(1)}, u32[]{:S(2)}, u32[]{:S(2)}) collective-permute-start(bf16[128,512]{1,0:T(8,128)(2,1)S(1)} %collective-permute-done.8), channel_id=1, source_target_pairs={{0,1},{1,2},{2,3},{3,4},{4,5},{5,6},{6,7},{7,8},{8,9},{9,10},{10,1... | collective-permute-start | bytes 393224 | tf_op jit(solution)/shard_map/ppermute | solution.py:17
  56.7 7.2 %collective-permute-start.11 = (bf16[128,512]{1,0:T(8,128)(2,1)S(1)}, bf16[128,512]{1,0:T(8,128)(2,1)S(1)}, u32[]{:S(2)}, u32[]{:S(2)}) collective-permute-start(bf16[128,512]{1,0:T(8,128)(2,1)S(1)} %collective-permute-done.9), channel_id=1, source_target_pairs={{0,15},{1,0},{2,1},{3,2},{4,3},{5,4},{6,5},{7,6},{8,7},{9,8},{10,9... | collective-permute-start | bytes 393224 | tf_op jit(solution)/shard_map/ppermute | solution.py:20
  63.9 7.1 %collective-permute-start.12 = (bf16[128,512]{1,0:T(8,128)(2,1)S(1)}, bf16[128,512]{1,0:T(8,128)(2,1)S(1)}, u32[]{:S(2)}, u32[]{:S(2)}) collective-permute-start(bf16[128,512]{1,0:T(8,128)(2,1)S(1)} %collective-permute-done.10), channel_id=1, source_target_pairs={{0,1},{1,2},{2,3},{3,4},{4,5},{5,6},{6,7},{7,8},{8,9},{9,10},{10,1... | collective-permute-start | bytes 393224 | tf_op jit(solution)/shard_map/ppermute | solution.py:17
  63.9 7.1 %collective-permute-start.13 = (bf16[128,512]{1,0:T(8,128)(2,1)S(1)}, bf16[128,512]{1,0:T(8,128)(2,1)S(1)}, u32[]{:S(2)}, u32[]{:S(2)}) collective-permute-start(bf16[128,512]{1,0:T(8,128)(2,1)S(1)} %collective-permute-done.11), channel_id=1, source_target_pairs={{0,15},{1,0},{2,1},{3,2},{4,3},{5,4},{6,5},{7,6},{8,7},{9,8},{10,9... | collective-permute-start | bytes 393224 | tf_op jit(solution)/shard_map/ppermute | solution.py:20
  71.0 7.1 %collective-permute-start.14 = (bf16[128,512]{1,0:T(8,128)(2,1)S(1)}, bf16[128,512]{1,0:T(8,128)(2,1)S(1)}, u32[]{:S(2)}, u32[]{:S(2)}) collective-permute-start(bf16[128,512]{1,0:T(8,128)(2,1)S(1)} %collective-permute-done.12), channel_id=1, source_target_pairs={{0,1},{1,2},{2,3},{3,4},{4,5},{5,6},{6,7},{7,8},{8,9},{9,10},{10,1... | collective-permute-start | bytes 393224 | tf_op jit(solution)/shard_map/ppermute | solution.py:17
  78.1 10.0 %slice-start = ((s8[16777216]{0:T(1024)(128)(4,1)}), s8[4194304]{0:T(1024)(128)(4,1)S(1)}, s32[]{:S(2)}) async-start(s8[16777216]{0:T(1024)(128)(4,1)} %bitcast.42), calls=%async_computation.4 | async-start | bytes 8388608
  79.6 8.5 %slice-start.1 = ((s8[16777216]{0:T(1024)(128)(4,1)}), s8[4194304]{0:T(1024)(128)(4,1)S(1)}, s32[]{:S(2)}) async-start(s8[16777216]{0:T(1024)(128)(4,1)} %bitcast.42), calls=%async_computation.5 | async-start | bytes 8388608
  79.6 8.5 %slice-start.2 = ((s8[16777216]{0:T(1024)(128)(4,1)}), s8[4194304]{0:T(1024)(128)(4,1)S(1)}, s32[]{:S(2)}) async-start(s8[16777216]{0:T(1024)(128)(4,1)} %bitcast.42), calls=%async_computation.6 | async-start | bytes 8388608
  79.6 9.5 %slice-start.3 = ((s8[16777216]{0:T(1024)(128)(4,1)}), s8[4194304]{0:T(1024)(128)(4,1)S(1)}, s32[]{:S(2)}) async-start(s8[16777216]{0:T(1024)(128)(4,1)} %bitcast.42), calls=%async_computation.7 | async-start | bytes 8388608
  79.6 9.5 %copy-start.5 = (bf16[128,1024]{1,0:T(8,128)(2,1)S(1)}, bf16[128,1024]{1,0:T(8,128)(2,1)}, u32[]{:S(2)}) copy-start(bf16[128,1024]{1,0:T(8,128)(2,1)} %param.8) | copy-start | bytes 786436
  96.7 147.3 %reduce-scatter.3.cloned.1.call-start = ((), (), s32[]{:S(2)}) async-start(), calls=%async_computation.2 | async-start | bytes 4456448 | tf_op jit(solution)/shard_map/reduce_scatter | solution.py:109
Sparse Core Ops, SparseCore 0:
  96.8 71.1 reduce-scatter.4
  172.3 71.6 reduce-scatter.2
